TPU v7x, 128 devices: a whole 4x4x4 slice. The times are simulated.
128 devices in a mesh: layer: 4 (over y_lo, core), shard: 32 (over z, y_hi, x).
Axes of the slice: x: 4, y: 4 (y_hi: 2, y_lo: 2; y = y_hi * 2 + y_lo), z: 4, core: 2. Of those that a mesh axis runs over, the one named last changes fastest.
Arguments:
- input_acts: bfloat16 [8, 16384, 5120], P('layer', 'shard'), may hold values from -6 to 6
- output_grads: bfloat16 [8, 16384, 1024], P('layer', 'shard'), may hold values from -6 to 6
- input_inverse: bfloat16 [8, 5120, 5120], P('layer', 'shard'), may hold values from -1 to 2, as said below
- output_inverse: bfloat16 [8, 1024, 1024], P('layer', 'shard'), may hold values from -1 to 2, as said below
- query_input: bfloat16 [8, 5120, 512], P(None, 'shard'), may hold values from -0.0048828125 to 0.0048828125
- query_output: bfloat16 [8, 1024, 512], P(None, 'shard'), may hold values from -0.1875 to 0.1875
- layer_order: int32 [8], replicated, may hold values from 0 to 7, each once
Outputs:
- scores: float32 [16384, 16], P('shard', 'layer')
Inputs may be any that keep to these rules, and one draw needn't show every extreme that they name: `input_inverse`: symmetric in its last two dimensions, with a unit-sized diagonal. `output_inverse`: symmetric in its last two dimensions, with a unit-sized diagonal.
All inputs are finite; a program needn't handle non-finite values.
Results may differ from a plain program's by a relative error of at most 0.0045.
Values may be sent and summed in bfloat16 or wider, within the bound.
A program may use at most 128 MiB of HBM per device.

v0:
```python
import jax
import jax.numpy as jnp
from jax import lax
from jax.sharding import PartitionSpec as P

QUERIES = 16


def joined_along(tiles, dim):
    dims = list(tiles.shape[1:])
    dims[dim] *= tiles.shape[0]
    return jnp.moveaxis(tiles, 0, dim).reshape(dims)


def sent_to_all(shard, axis):
    devices = lax.axis_size(axis)
    return lax.all_to_all(
        jnp.broadcast_to(shard[None], (devices, *shard.shape)), axis, 0, 0, tiled=True
    )


def gather_directly(shard, axis, dim):
    return joined_along(sent_to_all(shard, axis), dim)


def shards(
    input_acts, output_grads, input_inverse, output_inverse, query_input, query_output, layer_order
):
    depth = input_acts.shape[0]
    tokens = input_acts.shape[1]
    first = lax.axis_index("layer") * depth
    chosen_in = []
    chosen_out = []
    for position in range(depth):
        model_layer = layer_order[first + position]
        chosen_in.append(lax.dynamic_index_in_dim(query_input, model_layer, 0, keepdims=False))
        chosen_out.append(lax.dynamic_index_in_dim(query_output, model_layer, 0, keepdims=False))
    vectors_in = jnp.stack(chosen_in, axis=1)
    vectors_out = jnp.stack(chosen_out, axis=1)
    width = vectors_in.shape[2]
    whole_in = lax.all_gather(vectors_in, "shard", axis=0, tiled=True)
    folded_in = jnp.einsum(
        "jsk,kjn->sjn", input_inverse, whole_in, preferred_element_type=jnp.float32
    ).astype(jnp.bfloat16)
    columns = input_acts
    left = jnp.einsum(
        "jti,ijn->jtn",
        columns,
        lax.all_gather(folded_in, "shard", axis=0, tiled=True),
        preferred_element_type=jnp.float32,
    )
    whole_out = gather_directly(vectors_out, "shard", 0)
    folded_out = jnp.einsum(
        "jsk,kjn->sjn", output_inverse, whole_out, preferred_element_type=jnp.float32
    ).astype(jnp.bfloat16)
    columns = output_grads
    right = jnp.einsum(
        "jti,ijn->jtn",
        columns,
        gather_directly(folded_out, "shard", 0),
        preferred_element_type=jnp.float32,
    )
    product = (left * right).reshape(depth, tokens, QUERIES, width // QUERIES).sum(axis=(0, 3))
    return lax.psum_scatter(product, "layer", scatter_dimension=1, tiled=True)


def solution(mesh):
    in_specs = (
        P("layer", "shard", None),
        P("layer", "shard", None),
        P("layer", "shard", None),
        P("layer", "shard", None),
        P(None, "shard", None),
        P(None, "shard", None),
        P(),
    )
    out_specs = P("shard", "layer")
    return jax.shard_map(shards, mesh=mesh, in_specs=in_specs, out_specs=out_specs, check_vma=False)
```

profile of v0, /device:TPU:1, one launch (start us, length us, event | category | flops | bytes accessed | tf_op | source)
XLA Modules:
  0.0 326.5 jit_solution(4169752645969869274)
XLA Ops:
  6.5 0.0 copy-start
  6.5 0.0 all-gather.3.cloned.1.call-start
  6.5 1.4 fusion.2
  11.6 1.0 dynamic-slice_bitcast_fusion.1
  12.6 0.8 pad_maximum_fusion
  13.4 0.0 all-gather.3.cloned.1.call-update
  13.4 0.0 all-gather.5.cloned.1.call-start
  13.4 119.2 %all-gather.3.cloned.1.call-done = bf16[5120,2,512]{2,0,1:T(8,128)(2,1)} async-done(((bf16[160,2,512]{2,0,1:T(8,128)(2,1)}), bf16[5120,2,512]{2,0,1:T(8,128)(2,1)}) %all-gather.3.cloned.1.call-update) | async-done | bytes 10485776 | tf_op jit(solution)/shard_map/all_gather | solution.py:41
  132.7 0.0 copy-done
  132.7 6.6 %fusion = bf16[160,2,512]{2,0,1:T(8,128)(2,1)} fusion(bf16[2,160,5120]{2,1,0:T(8,128)(2,1)S(1)} %copy-done, bf16[5120,2,512]{2,0,1:T(8,128)(2,1)} %all-gather.3.cloned.1.call-done), kind=kOutput, calls=%fused_computation.2 | convolution fusion | flops 1677885440 | bytes 14090240 | tf_op jit(solution)/shard_map/jsk,kjn->sjn/dot_general | solution.py:42
  139.2 0.0 all-gather.5.cloned.1.call-update
  139.3 0.8 dynamic-slice_bitcast_fusion.3
  140.1 0.2 broadcast_in_dim.4
  140.3 36.1 %all_to_all.10 = bf16[32,32,2,512]{3,1,2,0:T(8,128)(2,1)S(1)} all-to-all(bf16[32,32,2,512]{3,1,2,0:T(8,128)(2,1)S(1)} %broadcast_in_dim.4), channel_id=1, replica_groups=mesh['layer'=4,'shard'=32] {'shard'}, dimensions={0} | all-to-all | bytes 4194304 | tf_op jit(solution)/shard_map/all_to_all | solution.py:17
  176.4 0.0 copy-start.1
  176.5 0.2 copy.13
  176.7 0.7 copy-done.1
  177.4 0.4 fusion.1
  177.8 1.6 broadcast_in_dim.5
  179.4 0.0 copy-start.2
  179.4 5.1 %all-to-all-start.1 = ((bf16[32,32,2,512]{3,1,2,0:T(8,128)(2,1)}), bf16[32,32,2,512]{3,1,2,0:T(8,128)(2,1)}, u32[]{:S(2)}, u32[]{:S(2)}) async-start(bf16[32,32,2,512]{3,1,2,0:T(8,128)(2,1)} %broadcast_in_dim.5), calls=%async_computation.1 | async-start | bytes 4194304 | tf_op jit(solution)/shard_map/all_to_all | solution.py:17
  184.5 0.0 copy-done.2
  184.5 0.6 dynamic-slice
  185.7 34.5 %all-to-all-done.1 = bf16[32,32,2,512]{3,1,2,0:T(8,128)(2,1)} async-done(((bf16[32,32,2,512]{3,1,2,0:T(8,128)(2,1)}), bf16[32,32,2,512]{3,1,2,0:T(8,128)(2,1)}, u32[]{:S(2)}, u32[]{:S(2)}) %all-to-all-start.1) | async-done | bytes 2097184 | tf_op jit(solution)/shard_map/all_to_all | solution.py:17
  220.2 3.2 copy.14
  223.4 66.7 %all-gather.5.cloned.1.call-done = bf16[5120,2,512]{2,0,1:T(8,128)(2,1)} async-done(((bf16[160,2,512]{2,0,1:T(8,128)(2,1)}), bf16[5120,2,512]{2,0,1:T(8,128)(2,1)}) %all-gather.5.cloned.1.call-update) | async-done | bytes 10485776 | tf_op jit(solution)/shard_map/all_gather | solution.py:49
  290.1 13.7 %fusion.3 = f32[2,512,512]{2,1,0:T(8,128)} fusion(bf16[5120,2,512]{2,0,1:T(8,128)(2,1)} %all-gather.5.cloned.1.call-done, bf16[2,512,5120]{2,1,0:T(8,128)(2,1)} %param.7), kind=kOutput, calls=%fused_computation.14 | convolution fusion | flops 5368709120 | bytes 23068672 | tf_op jit(solution)/shard_map/jti,ijn->jtn/dot_general | solution.py:46
  303.7 4.6 %multiply_reduce_fusion = f32[512,512]{1,0:T(8,128)S(1)} fusion(f32[2,512,512]{2,1,0:T(8,128)} %fusion.3, bf16[1024,2,512]{2,0,1:T(8,128)(2,1)} %bitcast.29, bf16[2,512,1024]{2,1,0:T(8,128)(2,1)} %param.8), kind=kOutput, calls=%fused_computation | convolution fusion | flops 1074528256 | bytes 7340032 | tf_op jit(solution)/shard_map/jti,ijn->jtn/dot_general | solution.py:57
  308.3 0.2 bitcast_reduce_fusion
  308.5 10.6 %all-reduce = f32[512,16]{0,1:T(8,128)S(1)} all-reduce(f32[512,16]{0,1:T(8,128)S(1)} %bitcast_reduce_fusion), channel_id=2, replica_groups=mesh['layer'=4,'shard'=32] {'layer'}, use_global_device_ids=true, to_apply=%region_2.3.clone | all-reduce | flops 8192 | bytes 65536
  319.0 0.6 constant_dynamic-slice_fusion
  (1 shorter events, 0.0 us)
Async XLA Ops:
  6.5 126.1 %copy-start = (bf16[2,160,5120]{2,1,0:T(8,128)(2,1)S(1)}, bf16[2,160,5120]{2,1,0:T(8,128)(2,1)}, u32[]{:S(2)}) copy-start(bf16[2,160,5120]{2,1,0:T(8,128)(2,1)} %param.9) | copy-start | bytes 9830404
  6.5 126.1 %all-gather.3.cloned.1.call-start = ((), (), s32[]{:S(2)}) async-start(), calls=%async_computation.2 | async-start | bytes 10813440 | tf_op jit(solution)/shard_map/all_gather | solution.py:41
  13.4 276.7 %all-gather.5.cloned.1.call-start = ((), (), s32[]{:S(2)}) async-start(), calls=%async_computation.3 | async-start | bytes 10813440 | tf_op jit(solution)/shard_map/all_gather | solution.py:49
  176.4 0.9 copy-start.1
  179.4 5.1 %copy-start.2 = (u32[128]{0:T(128)S(1)}, u32[128]{0:T(128)}, u32[]{:S(2)}) copy-start(u32[128]{0:T(128)} %constant.36) | copy-start | bytes 1540
  179.4 40.8 %all-to-all-start.1 = ((bf16[32,32,2,512]{3,1,2,0:T(8,128)(2,1)}), bf16[32,32,2,512]{3,1,2,0:T(8,128)(2,1)}, u32[]{:S(2)}, u32[]{:S(2)}) async-start(bf16[32,32,2,512]{3,1,2,0:T(8,128)(2,1)} %broadcast_in_dim.5), calls=%async_computation.1 | async-start | bytes 4194304 | tf_op jit(solution)/shard_map/all_to_all | solution.py:17
Sparse Core Ops, SparseCore 0:
  13.5 119.1 all-gather.2
  139.4 150.6 all-gather.4
where the time goes:
time: 327 us; the launch traced here: 326 us
  waiting for transfers between devices  220 us (67%)
  blocking collectives  46.7 us (14%)
  matrix products  25.3 us (8%)
  between operations  17.7 us (5%)
  local copies, waits for them, and re-layouts  10.3 us (3%)
  starting transfers between devices  5.12 us (2%)
    all_gather x1, waiting for transfers between devices, shards(): whole_in = lax.all_gather(vectors_in, 'shard', axis=0, tiled=True)  119 us
    all_gather x1, waiting for transfers between devices, shards(): lax.all_gather(folded_in, 'shard', axis=0, tiled=True)  66.7 us
    all_to_all x1, blocking collectives, sent_to_all(): lax.all_to_all(jnp.broadcast_to(shard[None], (devices, *shard.shape)), ax...  36.1 us
    all_to_all x1, waiting for transfers between devices, sent_to_all(): lax.all_to_all(jnp.broadcast_to(shard[None], (devices, *shard.shape)), ax...  34.5 us
    dot_general x1, matrix products, shards(): jnp.einsum('jti,ijn->jtn', columns, lax.all_gather(folded_in, 'shard', ax...  13.7 us
    unnamed x1, blocking collectives  10.6 us
    dot_general x1, matrix products, shards(): jnp.einsum('jsk,kjn->sjn', input_inverse, whole_in, preferred_element_typ...  6.58 us
  transfers between devices with their start and end apart: 3, of which 3 were waited for; matrix products, arithmetic and copies ran while one was open for 2% of the time, Pallas kernels for 0%

commit v1 on v0

--- a/solution.py
+++ b/solution.py
@@ -38,7 +38,9 @@
     vectors_in = jnp.stack(chosen_in, axis=1)
     vectors_out = jnp.stack(chosen_out, axis=1)
     width = vectors_in.shape[2]
-    whole_in = lax.all_gather(vectors_in, "shard", axis=0, tiled=True)
+    whole_in = jnp.concatenate(
+        lax.all_to_all(jnp.stack([vectors_in] * lax.axis_size("shard")), "shard", 0, 0), axis=0
+    )
     folded_in = jnp.einsum(
         "jsk,kjn->sjn", input_inverse, whole_in, preferred_element_type=jnp.float32
     ).astype(jnp.bfloat16)

time: 327 us -> 351 us (1.073)
  blocking collectives: 46.7 us -> 176 us
  waiting for transfers between devices: 220 us -> 103 us
  local copies, waits for them, and re-layouts: 10.3 us -> 22.9 us
    all_to_all x0 -> x1, blocking collectives: none -> 129 us  [shards(): lax.all_to_all(jnp.stack([vectors_in] * lax.axis_size('shard')), 'shard',...]
    all_gather x1 -> x0, waiting for transfers between devices: 119 us -> none  [shards(): whole_in = lax.all_gather(vectors_in, 'shard', axis=0, tiled=True)]
    all_to_all x0 -> x1, local copies, waits for them, and re-layouts: none -> 9.05 us  [shards(): lax.all_to_all(jnp.stack([vectors_in] * lax.axis_size('shard')), 'shard',...]
    another operation x0 -> x1, local copies, waits for them, and re-layouts: none -> 5.1 us  [shards(): jnp.stack([vectors_in] * lax.axis_size('shard'))]
  transfers between devices with their start and end apart: 3 -> 2, of which waited for: 3 -> 2; matrix products, arithmetic and copies ran while one was open for 2% -> 2% of each run, Pallas kernels for 0% -> 0%
where the time goes in v1:
time: 351 us
  blocking collectives  176 us (50%)
  waiting for transfers between devices  103 us (29%)
  matrix products  25.4 us (7%)
  local copies, waits for them, and re-layouts  22.9 us (7%)
  between operations  17.9 us (5%)
  starting transfers between devices  4.82 us (1%)
    all_to_all x1, blocking collectives, shards(): lax.all_to_all(jnp.stack([vectors_in] * lax.axis_size('shard')), 'shard',...  129 us
    all_gather x1, waiting for transfers between devices, shards(): lax.all_gather(folded_in, 'shard', axis=0, tiled=True)  68.4 us
    all_to_all x1, blocking collectives, sent_to_all(): lax.all_to_all(jnp.broadcast_to(shard[None], (devices, *shard.shape)), ax...  36.3 us
    all_to_all x1, waiting for transfers between devices, sent_to_all(): lax.all_to_all(jnp.broadcast_to(shard[None], (devices, *shard.shape)), ax...  34.9 us
    dot_general x1, matrix products, shards(): jnp.einsum('jti,ijn->jtn', columns, lax.all_gather(folded_in, 'shard', ax...  13.7 us
    unnamed x1, blocking collectives  10.6 us
    all_to_all x1, local copies, waits for them, and re-layouts, shards(): lax.all_to_all(jnp.stack([vectors_in] * lax.axis_size('shard')), 'shard',...  9.05 us
  transfers between devices with their start and end apart: 2, of which 2 were waited for; matrix products, arithmetic and copies ran while one was open for 2% of the time, Pallas kernels for 0%

profile of v1, /device:TPU:1, one launch (start us, length us, event | category | flops | bytes accessed | tf_op | source)
XLA Modules:
  0.0 350.9 jit_solution(5407998632939976864)
XLA Ops:
  6.5 0.0 copy-start
  6.5 0.0 all-gather.2.cloned.1.call-start
  6.5 1.4 fusion.2
  11.7 1.0 dynamic-slice_bitcast_fusion.1
  12.8 5.1 %stack.17 = bf16[32,160,2,512]{3,1,2,0:T(8,128)(2,1)} broadcast(bf16[160,2,512]{2,0,1:T(8,128)(2,1)S(1)} %pad_maximum_fusion), dimensions={1,2,3} | broadcast | bytes 10813440 | tf_op jit(solution)/shard_map/stack | solution.py:42
  17.9 129.5 %all_to_all.15 = bf16[32,160,2,512]{3,1,2,0:T(8,128)(2,1)} all-to-all(bf16[32,160,2,512]{3,1,2,0:T(8,128)(2,1)} %stack.17), channel_id=1, replica_groups=mesh['layer'=4,'shard'=32] {'shard'}, dimensions={0} | all-to-all | bytes 20971520 | tf_op jit(solution)/shard_map/all_to_all | solution.py:42
  147.4 9.1 %copy.18 = bf16[32,160,2,512]{3,1,0,2:T(8,128)(2,1)} copy(bf16[32,160,2,512]{3,1,2,0:T(8,128)(2,1)} %all_to_all.15) | data formatting | bytes 20971520 | tf_op jit(solution)/shard_map/all_to_all | solution.py:42
  156.5 0.0 copy-done
  156.5 6.6 %fusion = bf16[160,2,512]{2,0,1:T(8,128)(2,1)} fusion(bf16[2,160,5120]{2,1,0:T(8,128)(2,1)S(1)} %copy-done, bf16[5120,2,512]{2,0,1:T(8,128)(2,1)} %bitcast.30), kind=kOutput, calls=%fused_computation.2 | convolution fusion | flops 1677885440 | bytes 14090240 | tf_op jit(solution)/shard_map/jsk,kjn->sjn/dot_general | solution.py:44
  163.0 0.0 all-gather.2.cloned.1.call-update
  163.1 0.8 dynamic-slice_bitcast_fusion.3
  163.9 0.2 broadcast_in_dim.4
  164.1 36.3 %all_to_all.16 = bf16[32,32,2,512]{3,1,2,0:T(8,128)(2,1)S(1)} all-to-all(bf16[32,32,2,512]{3,1,2,0:T(8,128)(2,1)S(1)} %broadcast_in_dim.4), channel_id=1, replica_groups=mesh['layer'=4,'shard'=32] {'shard'}, dimensions={0} | all-to-all | bytes 4194304 | tf_op jit(solution)/shard_map/all_to_all | solution.py:17
  200.4 0.0 copy-start.2
  200.4 0.2 copy.19
  200.7 0.7 copy-done.2
  201.3 0.4 fusion.1
  201.8 1.6 broadcast_in_dim.5
  203.4 0.0 copy-start.3
  203.4 4.8 %all-to-all-start.2 = ((bf16[32,32,2,512]{3,1,2,0:T(8,128)(2,1)}), bf16[32,32,2,512]{3,1,2,0:T(8,128)(2,1)S(1)}, u32[]{:S(2)}, u32[]{:S(2)}) async-start(bf16[32,32,2,512]{3,1,2,0:T(8,128)(2,1)} %broadcast_in_dim.5), calls=%async_computation.2 | async-start | bytes 4194304 | tf_op jit(solution)/shard_map/all_to_all | solution.py:17
  208.2 0.0 copy-done.3
  208.2 0.6 dynamic-slice
  209.4 34.9 %all-to-all-done.2 = bf16[32,32,2,512]{3,1,2,0:T(8,128)(2,1)S(1)} async-done(((bf16[32,32,2,512]{3,1,2,0:T(8,128)(2,1)}), bf16[32,32,2,512]{3,1,2,0:T(8,128)(2,1)S(1)}, u32[]{:S(2)}, u32[]{:S(2)}) %all-to-all-start.2) | async-done | bytes 2097184 | tf_op jit(solution)/shard_map/all_to_all | solution.py:17
  244.4 1.6 copy.20
  245.9 68.4 %all-gather.2.cloned.1.call-done = bf16[5120,2,512]{2,0,1:T(8,128)(2,1)} async-done(((bf16[160,2,512]{2,0,1:T(8,128)(2,1)}), bf16[5120,2,512]{2,0,1:T(8,128)(2,1)}) %all-gather.2.cloned.1.call-update) | async-done | bytes 10485776 | tf_op jit(solution)/shard_map/all_gather | solution.py:51
  314.3 13.7 %fusion.3 = f32[2,512,512]{2,1,0:T(8,128)} fusion(bf16[5120,2,512]{2,0,1:T(8,128)(2,1)} %all-gather.2.cloned.1.call-done, bf16[2,512,5120]{2,1,0:T(8,128)(2,1)} %param.7), kind=kOutput, calls=%fused_computation.14 | convolution fusion | flops 5368709120 | bytes 23068672 | tf_op jit(solution)/shard_map/jti,ijn->jtn/dot_general | solution.py:48
  328.0 0.0 copy-start.1
  328.0 4.7 %multiply_reduce_fusion = f32[512,512]{1,0:T(8,128)S(1)} fusion(f32[2,512,512]{2,1,0:T(8,128)} %fusion.3, bf16[1024,2,512]{2,0,1:T(8,128)(2,1)} %bitcast.31, bf16[2,512,1024]{2,1,0:T(8,128)(2,1)} %param.8), kind=kOutput, calls=%fused_computation | convolution fusion | flops 1074528256 | bytes 7340032 | tf_op jit(solution)/shard_map/jti,ijn->jtn/dot_general | solution.py:59
  332.7 0.2 bitcast_reduce_fusion
  332.9 10.6 %all-reduce = f32[512,16]{0,1:T(8,128)S(1)} all-reduce(f32[512,16]{0,1:T(8,128)S(1)} %bitcast_reduce_fusion), channel_id=2, replica_groups=mesh['layer'=4,'shard'=32] {'layer'}, use_global_device_ids=true, to_apply=%region_2.3.clone | all-reduce | flops 8192 | bytes 65536
  343.4 0.6 constant_dynamic-slice_fusion
  344.0 0.0 copy-done.1
  (2 shorter events, 0.0 us)
Async XLA Ops:
  6.5 149.9 %copy-start = (bf16[2,160,5120]{2,1,0:T(8,128)(2,1)S(1)}, bf16[2,160,5120]{2,1,0:T(8,128)(2,1)}, u32[]{:S(2)}) copy-start(bf16[2,160,5120]{2,1,0:T(8,128)(2,1)} %param.9) | copy-start | bytes 9830404
  6.5 307.8 %all-gather.2.cloned.1.call-start = ((), (), s32[]{:S(2)}) async-start(), calls=%async_computation.3 | async-start | bytes 10813440 | tf_op jit(solution)/shard_map/all_gather | solution.py:51
  200.4 0.9 copy-start.2
  203.4 4.8 %copy-start.3 = (u32[128]{0:T(128)S(1)}, u32[128]{0:T(128)}, u32[]{:S(2)}) copy-start(u32[128]{0:T(128)} %constant.36) | copy-start | bytes 1540
  203.4 41.0 %all-to-all-start.2 = ((bf16[32,32,2,512]{3,1,2,0:T(8,128)(2,1)}), bf16[32,32,2,512]{3,1,2,0:T(8,128)(2,1)S(1)}, u32[]{:S(2)}, u32[]{:S(2)}) async-start(bf16[32,32,2,512]{3,1,2,0:T(8,128)(2,1)} %broadcast_in_dim.5), calls=%async_computation.2 | async-start | bytes 4194304 | tf_op jit(solution)/shard_map/all_to_all | solution.py:17
  328.0 16.1 %copy-start.1 = (bf16[2,160,5120]{2,1,0:T(8,128)(2,1)S(1)}, bf16[2,160,5120]{2,1,0:T(8,128)(2,1)}, u32[]{:S(2)}) copy-start(bf16[2,160,5120]{2,1,0:T(8,128)(2,1)} %param.9) | copy-start | bytes 9830404
Sparse Core Ops, SparseCore 0:
  163.2 151.0 all-gather.1
